TPU v7x, 256 devices: a whole 4x4x8 slice. The times are simulated.
256 devices in a mesh: sec: 4 (over x_hi, core), dom: 64 (over y, z, x_lo).
Axes of the slice: x: 4 (x_hi: 2, x_lo: 2; x = x_hi * 2 + x_lo), y: 4, z: 8, core: 2. Of those that a mesh axis runs over, the one named last changes fastest.
Arguments:
- actuator_fields: float32 [16, 512, 4096], P(None, 'dom', 'sec'), may hold values from -6 to 6
- sensor_fields: float32 [8, 512, 4096], P(None, 'dom', 'sec'), may hold values from -6 to 6
- region_ids: int32 [512, 4096], P('dom', 'sec'), may hold values from 0 to 15
- stiffness_table: float32 [16], replicated, may hold values from 1 to 4
- density_table: float32 [16], replicated, may hold values from 1 to 2
- supported: int32 [10, 64, 32], P(None, 'dom', 'sec'), may hold values 0 or 1
Outputs:
- final_position: float32 [24, 512, 4096], P(None, 'dom', 'sec')
- cross: float32 [160, 80], P('sec')
All inputs are finite; a program needn't handle non-finite values. No bound on the sum of `supported` on one device may be relied on, other than what follows from the above.
Results may differ from a plain program's by a relative error of at most 0.0028.
Values sent between devices are 32-bit elements; how exact they have to be, the bound alone decides.
No kernel may reach another device: no remote copies, remote signals or barrier semaphores. Data moves between devices by JAX's collectives and lax.ppermute only.
A program may use at most 64 MiB of HBM per device.

v0:
```python
import math
import jax
import jax.numpy as jnp
from jax import lax
from jax.sharding import PartitionSpec as P

TILE_Y = 128
ACT = 16
SNAPS = 10


def padded_2(cells, sides, width):
    for axis, dim in sides:
        count = lax.axis_size(axis)
        ends = count - 1
        head = lax.slice_in_dim(cells, 0, width, axis=dim)
        tail = lax.slice_in_dim(cells, cells.shape[dim] - width, cells.shape[dim], axis=dim)
        cells = jnp.concatenate(
            [
                lax.ppermute(tail, axis, [(i, (i + 1) % count) for i in range(ends)]),
                cells,
                lax.ppermute(head, axis, [((i + 1) % count, i) for i in range(ends)]),
            ],
            axis=dim,
        )
    return cells


def divergence(padded, stiff_pad):
    rows = padded.shape[-2] - 2
    cols = padded.shape[-1] - 2
    centre = padded[..., 1 : 1 + rows, 1 : 1 + cols]
    stiff_centre = stiff_pad[1 : 1 + rows, 1 : 1 + cols]
    total = jnp.zeros_like(centre)
    for first, second in ((0, 1), (2, 1), (1, 0), (1, 2)):
        nearby = padded[..., first : first + rows, second : second + cols]
        stiff_near = stiff_pad[first : first + rows, second : second + cols]
        total = total + 0.5 * (stiff_centre + stiff_near) * (nearby - centre)
    return total


def lookup(region_ids, table):
    labels = jnp.arange(table.shape[0], dtype=jnp.int32)
    match = (region_ids[None, :, :] == labels[:, None, None]).astype(jnp.float32)
    return jnp.sum(match * table[:, None, None], axis=0)


def body(actuator_fields, sensor_fields, region_ids, stiffness_table, density_table, supported):
    stiffness = lookup(region_ids, stiffness_table)
    inv_mass = 1.0 / lookup(region_ids, density_table)
    depth = 1
    stiff_pad, mass_pad = (
        padded_2(stiffness, (("sec", 1), ("dom", 0)), depth),
        padded_2(inv_mass, (("sec", 1), ("dom", 0)), depth),
    )
    velocity = jnp.concatenate([actuator_fields, sensor_fields], 0) * inv_mass
    position = jnp.zeros_like(velocity)
    count = velocity.shape[0]
    rows, cols = stiffness.shape
    frames = jnp.zeros((count, SNAPS, 2, rows, cols), jnp.bfloat16)

    def one_step(position, velocity):
        padded = padded_2(position, (("sec", 2), ("dom", 1)), 1)
        velocity = velocity + 0.35 * inv_mass * divergence(padded, stiff_pad)
        return (position + 0.35 * velocity, velocity)

    def advance(position, velocity):
        position, velocity = one_step(position, velocity)
        return one_step(position, velocity)

    def pair_step(index, carry):
        position, velocity, frames = carry
        position, velocity = advance(position, velocity)
        mask_row = lax.dynamic_index_in_dim(supported, index, 0, keepdims=False)
        cells = jnp.repeat(mask_row, TILE_Y, axis=1).astype(jnp.float32)
        frame = jnp.stack([position * cells, velocity * cells], 1).astype(jnp.bfloat16)
        frames = lax.dynamic_update_slice_in_dim(frames, frame[:, None], index, 1)
        return (position, velocity, frames)

    position, velocity, frames = lax.fori_loop(0, SNAPS, pair_step, (position, velocity, frames))
    flat_frames = frames.reshape(count * SNAPS, 2 * rows * cols)
    primal = flat_frames[: ACT * SNAPS]
    adjoint = flat_frames[ACT * SNAPS :]
    local = lax.dot_general(
        primal, adjoint, (((1,), (1,)), ((), ())), preferred_element_type=jnp.float32
    )
    factor = 1.0 / math.sqrt(rows * cols * lax.axis_size("sec") * lax.axis_size("dom"))
    total = lax.psum(local, ("sec", "dom"))
    share = local.shape[0] // lax.axis_size("sec")
    block = lax.dynamic_slice_in_dim(total, lax.axis_index("sec") * share, share, 0)
    return (position, block * factor)


def solution(mesh):
    in_specs = (
        P(None, "dom", "sec"),
        P(None, "dom", "sec"),
        P("dom", "sec"),
        P(),
        P(),
        P(None, "dom", "sec"),
    )
    out_specs = (P(None, "dom", "sec"), P("sec", None))
    return jax.shard_map(body, mesh=mesh, in_specs=in_specs, out_specs=out_specs, check_vma=False)
```

profile of v0, /device:TPU:1, one launch (start us, length us, event | category | flops | bytes accessed | tf_op | source)
XLA Modules:
  0.0 726.7 jit_solution(2190407411875545413)
XLA Ops:
  19.1 551.6 %while.20 = (s32[]{:T(128)}, f32[24,8,1024]{2,1,0:T(8,128)}, f32[24,8,1024]{2,1,0:T(8,128)S(1)}, bf16[24,10,2,8,1024]{4,3,0,2,1:T(8,128)(2,1)}, f32[8,1024]{1,0:...) while((s32[]{:T(128)}, f32[24,8,1024]{2,1,0:T(8,128)}, ...), condition=%wide.region_3.4_spmd.clone, body=%wide.region_2.3_spmd.clone.sunk | while | flops 13410315 | bytes 20697064 | solution.py:80
  21.3 6.1 collective-permute-start.1
  43.4 6.1 collective-permute-start.5
  64.7 5.6 fusion.52
  74.6 6.8 collective-permute-start.1
  119.2 5.6 fusion.52
  129.0 6.5 collective-permute-start.1
  173.4 5.6 fusion.52
  183.2 6.5 collective-permute-start.1
  206.7 6.4 collective-permute-start.5
  228.3 5.6 fusion.52
  238.1 6.8 collective-permute-start.1
  282.7 5.6 fusion.52
  292.6 6.5 collective-permute-start.1
  316.0 6.1 collective-permute-start.5
  337.5 5.6 fusion.52
  347.4 6.5 collective-permute-start.1
  369.7 6.1 collective-permute-start.5
  383.3 8.3 %collective-permute-start.7 = (f32[24,1,1026]{2,1,0:T(1,128)}, f32[24,1,1026]{2,1,0:T(1,128)}, u32[]{:S(2)}, u32[]{:S(2)}) collective-permute-start(f32[24,1,1026]{2,1,0:T(1,128)} %get-tuple-element.423), channel_id=1, source_target_pairs={{0,1},{1,2},{2,3},{3,4},{4,5},{5,6},{6,7},{7,8},{8,9},{9,10},{10,1... | collective-permute-start | bytes 295496 | tf_op jit(solution)/shard_map/while/body/eval_jaxpr/ppermute | solution.py:20
  394.2 5.6 fusion.52
  404.0 6.5 collective-permute-start.1
  426.3 6.1 collective-permute-start.5
  440.0 8.3 %collective-permute-start.7 = (f32[24,1,1026]{2,1,0:T(1,128)}, f32[24,1,1026]{2,1,0:T(1,128)}, u32[]{:S(2)}, u32[]{:S(2)}) collective-permute-start(f32[24,1,1026]{2,1,0:T(1,128)} %get-tuple-element.423), channel_id=1, source_target_pairs={{0,1},{1,2},{2,3},{3,4},{4,5},{5,6},{6,7},{7,8},{8,9},{9,10},{10,1... | collective-permute-start | bytes 295496 | tf_op jit(solution)/shard_map/while/body/eval_jaxpr/ppermute | solution.py:20
  460.6 6.5 collective-permute-start.1
  482.9 6.1 collective-permute-start.5
  496.6 9.4 %collective-permute-start.7 = (f32[24,1,1026]{2,1,0:T(1,128)}, f32[24,1,1026]{2,1,0:T(1,128)}, u32[]{:S(2)}, u32[]{:S(2)}) collective-permute-start(f32[24,1,1026]{2,1,0:T(1,128)} %get-tuple-element.423), channel_id=1, source_target_pairs={{0,1},{1,2},{2,3},{3,4},{4,5},{5,6},{6,7},{7,8},{8,9},{9,10},{10,1... | collective-permute-start | bytes 295496 | tf_op jit(solution)/shard_map/while/body/eval_jaxpr/ppermute | solution.py:20
  507.5 5.6 fusion.52
  517.4 7.5 %collective-permute-start.1 = (f32[24,8,1]{2,1,0:T(8,128)S(1)}, f32[24,8,1]{2,1,0:T(8,128)S(1)}, u32[]{:S(2)}, u32[]{:S(2)}) collective-permute-start(f32[24,8,1]{2,1,0:T(8,128)S(1)} %get-tuple-element.414), channel_id=1, source_target_pairs={{0,64},{64,128},{128,192},{1,65},{65,129},{129,193},{2,66},{66,130... | collective-permute-start | bytes 2312 | tf_op jit(solution)/shard_map/while/body/eval_jaxpr/ppermute | solution.py:20
  540.6 7.5 %collective-permute-start.5 = (f32[24,8,1]{2,1,0:T(8,128)S(1)}, f32[24,8,1]{2,1,0:T(8,128)}, u32[]{:S(2)}, u32[]{:S(2)}) collective-permute-start(f32[24,8,1]{2,1,0:T(8,128)S(1)} %get-tuple-element.421), channel_id=1, source_target_pairs={{0,64},{64,128},{128,192},{1,65},{65,129},{129,193},{2,66},{66,130... | collective-permute-start | bytes 2312 | tf_op jit(solution)/shard_map/while/body/eval_jaxpr/ppermute | solution.py:20
  555.7 6.5 collective-permute-start.7
  579.3 8.9 %slice.229 = bf16[160,16384]{1,0:T(8,128)(2,1)} reshape(bf16[16,10,2,8,1024]{4,3,2,1,0:T(8,128)(2,1)} %copy.13) | data formatting | bytes 10485760 | tf_op jit(solution)/shard_map/slice | solution.py:82
  597.9 128.1 %psum.7 = f32[160,80]{1,0:T(8,128)S(1)} all-reduce(f32[160,80]{1,0:T(8,128)S(1)} %fusion.39), channel_id=1, replica_groups=mesh['sec'=4,'dom'=64] {'sec','dom'}, use_global_device_ids=true, to_apply=%region_4.5 | all-reduce | flops 12800 | bytes 102400 | tf_op jit(solution)/shard_map/psum | solution.py:88
  (356 shorter events, 400.2 us)
Async XLA Ops:
  19.2 11.0 %collective-permute-start = (f32[24,8,1]{2,1,0:T(8,128)S(1)}, f32[24,8,1]{2,1,0:T(8,128)S(1)}, u32[]{:S(2)}, u32[]{:S(2)}) collective-permute-start(f32[24,8,1]{2,1,0:T(8,128)S(1)} %get-tuple-element.412), channel_id=1, source_target_pairs={{64,0},{128,64},{192,128},{65,1},{129,65},{193,129},{66,2},{130,66... | collective-permute-start | bytes 2312 | tf_op jit(solution)/shard_map/while/body/eval_jaxpr/ppermute | solution.py:22
  41.5 9.3 %collective-permute-start.4 = (f32[24,8,1]{2,1,0:T(8,128)S(1)}, f32[24,8,1]{2,1,0:T(8,128)}, u32[]{:S(2)}, u32[]{:S(2)}) collective-permute-start(f32[24,8,1]{2,1,0:T(8,128)S(1)} %get-tuple-element.420), channel_id=1, source_target_pairs={{64,0},{128,64},{192,128},{65,1},{129,65},{193,129},{66,2},{130,66... | collective-permute-start | bytes 2312 | tf_op jit(solution)/shard_map/while/body/eval_jaxpr/ppermute | solution.py:22
  72.6 11.5 %collective-permute-start = (f32[24,8,1]{2,1,0:T(8,128)S(1)}, f32[24,8,1]{2,1,0:T(8,128)S(1)}, u32[]{:S(2)}, u32[]{:S(2)}) collective-permute-start(f32[24,8,1]{2,1,0:T(8,128)S(1)} %get-tuple-element.412), channel_id=1, source_target_pairs={{64,0},{128,64},{192,128},{65,1},{129,65},{193,129},{66,2},{130,66... | collective-permute-start | bytes 2312 | tf_op jit(solution)/shard_map/while/body/eval_jaxpr/ppermute | solution.py:22
  74.6 9.6 %collective-permute-start.1 = (f32[24,8,1]{2,1,0:T(8,128)S(1)}, f32[24,8,1]{2,1,0:T(8,128)S(1)}, u32[]{:S(2)}, u32[]{:S(2)}) collective-permute-start(f32[24,8,1]{2,1,0:T(8,128)S(1)} %get-tuple-element.414), channel_id=1, source_target_pairs={{0,64},{64,128},{128,192},{1,65},{65,129},{129,193},{2,66},{66,130... | collective-permute-start | bytes 2312 | tf_op jit(solution)/shard_map/while/body/eval_jaxpr/ppermute | solution.py:20
  127.1 11.2 %collective-permute-start = (f32[24,8,1]{2,1,0:T(8,128)S(1)}, f32[24,8,1]{2,1,0:T(8,128)S(1)}, u32[]{:S(2)}, u32[]{:S(2)}) collective-permute-start(f32[24,8,1]{2,1,0:T(8,128)S(1)} %get-tuple-element.412), channel_id=1, source_target_pairs={{64,0},{128,64},{192,128},{65,1},{129,65},{193,129},{66,2},{130,66... | collective-permute-start | bytes 2312 | tf_op jit(solution)/shard_map/while/body/eval_jaxpr/ppermute | solution.py:22
  129.0 9.3 %collective-permute-start.1 = (f32[24,8,1]{2,1,0:T(8,128)S(1)}, f32[24,8,1]{2,1,0:T(8,128)S(1)}, u32[]{:S(2)}, u32[]{:S(2)}) collective-permute-start(f32[24,8,1]{2,1,0:T(8,128)S(1)} %get-tuple-element.414), channel_id=1, source_target_pairs={{0,64},{64,128},{128,192},{1,65},{65,129},{129,193},{2,66},{66,130... | collective-permute-start | bytes 2312 | tf_op jit(solution)/shard_map/while/body/eval_jaxpr/ppermute | solution.py:20
  181.3 11.2 %collective-permute-start = (f32[24,8,1]{2,1,0:T(8,128)S(1)}, f32[24,8,1]{2,1,0:T(8,128)S(1)}, u32[]{:S(2)}, u32[]{:S(2)}) collective-permute-start(f32[24,8,1]{2,1,0:T(8,128)S(1)} %get-tuple-element.412), channel_id=1, source_target_pairs={{64,0},{128,64},{192,128},{65,1},{129,65},{193,129},{66,2},{130,66... | collective-permute-start | bytes 2312 | tf_op jit(solution)/shard_map/while/body/eval_jaxpr/ppermute | solution.py:22
  183.2 9.3 %collective-permute-start.1 = (f32[24,8,1]{2,1,0:T(8,128)S(1)}, f32[24,8,1]{2,1,0:T(8,128)S(1)}, u32[]{:S(2)}, u32[]{:S(2)}) collective-permute-start(f32[24,8,1]{2,1,0:T(8,128)S(1)} %get-tuple-element.414), channel_id=1, source_target_pairs={{0,64},{64,128},{128,192},{1,65},{65,129},{129,193},{2,66},{66,130... | collective-permute-start | bytes 2312 | tf_op jit(solution)/shard_map/while/body/eval_jaxpr/ppermute | solution.py:20
  204.8 9.5 %collective-permute-start.4 = (f32[24,8,1]{2,1,0:T(8,128)S(1)}, f32[24,8,1]{2,1,0:T(8,128)}, u32[]{:S(2)}, u32[]{:S(2)}) collective-permute-start(f32[24,8,1]{2,1,0:T(8,128)S(1)} %get-tuple-element.420), channel_id=1, source_target_pairs={{64,0},{128,64},{192,128},{65,1},{129,65},{193,129},{66,2},{130,66... | collective-permute-start | bytes 2312 | tf_op jit(solution)/shard_map/while/body/eval_jaxpr/ppermute | solution.py:22
  236.2 11.5 %collective-permute-start = (f32[24,8,1]{2,1,0:T(8,128)S(1)}, f32[24,8,1]{2,1,0:T(8,128)S(1)}, u32[]{:S(2)}, u32[]{:S(2)}) collective-permute-start(f32[24,8,1]{2,1,0:T(8,128)S(1)} %get-tuple-element.412), channel_id=1, source_target_pairs={{64,0},{128,64},{192,128},{65,1},{129,65},{193,129},{66,2},{130,66... | collective-permute-start | bytes 2312 | tf_op jit(solution)/shard_map/while/body/eval_jaxpr/ppermute | solution.py:22
  238.1 9.6 %collective-permute-start.1 = (f32[24,8,1]{2,1,0:T(8,128)S(1)}, f32[24,8,1]{2,1,0:T(8,128)S(1)}, u32[]{:S(2)}, u32[]{:S(2)}) collective-permute-start(f32[24,8,1]{2,1,0:T(8,128)S(1)} %get-tuple-element.414), channel_id=1, source_target_pairs={{0,64},{64,128},{128,192},{1,65},{65,129},{129,193},{2,66},{66,130... | collective-permute-start | bytes 2312 | tf_op jit(solution)/shard_map/while/body/eval_jaxpr/ppermute | solution.py:20
  290.6 11.2 %collective-permute-start = (f32[24,8,1]{2,1,0:T(8,128)S(1)}, f32[24,8,1]{2,1,0:T(8,128)S(1)}, u32[]{:S(2)}, u32[]{:S(2)}) collective-permute-start(f32[24,8,1]{2,1,0:T(8,128)S(1)} %get-tuple-element.412), channel_id=1, source_target_pairs={{64,0},{128,64},{192,128},{65,1},{129,65},{193,129},{66,2},{130,66... | collective-permute-start | bytes 2312 | tf_op jit(solution)/shard_map/while/body/eval_jaxpr/ppermute | solution.py:22
  292.6 9.3 %collective-permute-start.1 = (f32[24,8,1]{2,1,0:T(8,128)S(1)}, f32[24,8,1]{2,1,0:T(8,128)S(1)}, u32[]{:S(2)}, u32[]{:S(2)}) collective-permute-start(f32[24,8,1]{2,1,0:T(8,128)S(1)} %get-tuple-element.414), channel_id=1, source_target_pairs={{0,64},{64,128},{128,192},{1,65},{65,129},{129,193},{2,66},{66,130... | collective-permute-start | bytes 2312 | tf_op jit(solution)/shard_map/while/body/eval_jaxpr/ppermute | solution.py:20
  314.1 9.2 %collective-permute-start.4 = (f32[24,8,1]{2,1,0:T(8,128)S(1)}, f32[24,8,1]{2,1,0:T(8,128)}, u32[]{:S(2)}, u32[]{:S(2)}) collective-permute-start(f32[24,8,1]{2,1,0:T(8,128)S(1)} %get-tuple-element.420), channel_id=1, source_target_pairs={{64,0},{128,64},{192,128},{65,1},{129,65},{193,129},{66,2},{130,66... | collective-permute-start | bytes 2312 | tf_op jit(solution)/shard_map/while/body/eval_jaxpr/ppermute | solution.py:22
  345.4 11.2 %collective-permute-start = (f32[24,8,1]{2,1,0:T(8,128)S(1)}, f32[24,8,1]{2,1,0:T(8,128)S(1)}, u32[]{:S(2)}, u32[]{:S(2)}) collective-permute-start(f32[24,8,1]{2,1,0:T(8,128)S(1)} %get-tuple-element.412), channel_id=1, source_target_pairs={{64,0},{128,64},{192,128},{65,1},{129,65},{193,129},{66,2},{130,66... | collective-permute-start | bytes 2312 | tf_op jit(solution)/shard_map/while/body/eval_jaxpr/ppermute | solution.py:22
  347.4 9.3 %collective-permute-start.1 = (f32[24,8,1]{2,1,0:T(8,128)S(1)}, f32[24,8,1]{2,1,0:T(8,128)S(1)}, u32[]{:S(2)}, u32[]{:S(2)}) collective-permute-start(f32[24,8,1]{2,1,0:T(8,128)S(1)} %get-tuple-element.414), channel_id=1, source_target_pairs={{0,64},{64,128},{128,192},{1,65},{65,129},{129,193},{2,66},{66,130... | collective-permute-start | bytes 2312 | tf_op jit(solution)/shard_map/while/body/eval_jaxpr/ppermute | solution.py:20
  367.8 9.3 %collective-permute-start.4 = (f32[24,8,1]{2,1,0:T(8,128)S(1)}, f32[24,8,1]{2,1,0:T(8,128)}, u32[]{:S(2)}, u32[]{:S(2)}) collective-permute-start(f32[24,8,1]{2,1,0:T(8,128)S(1)} %get-tuple-element.420), channel_id=1, source_target_pairs={{64,0},{128,64},{192,128},{65,1},{129,65},{193,129},{66,2},{130,66... | collective-permute-start | bytes 2312 | tf_op jit(solution)/shard_map/while/body/eval_jaxpr/ppermute | solution.py:22
  382.0 10.3 %collective-permute-start.6 = (f32[24,1,1026]{2,1,0:T(1,128)}, f32[24,1,1026]{2,1,0:T(1,128)}, u32[]{:S(2)}, u32[]{:S(2)}) collective-permute-start(f32[24,1,1026]{2,1,0:T(1,128)} %get-tuple-element.422), channel_id=1, source_target_pairs={{1,0},{2,1},{3,2},{4,3},{5,4},{6,5},{7,6},{8,7},{9,8},{10,9},{11,1... | collective-permute-start | bytes 295496 | tf_op jit(solution)/shard_map/while/body/eval_jaxpr/ppermute | solution.py:22
  383.3 10.8 %collective-permute-start.7 = (f32[24,1,1026]{2,1,0:T(1,128)}, f32[24,1,1026]{2,1,0:T(1,128)}, u32[]{:S(2)}, u32[]{:S(2)}) collective-permute-start(f32[24,1,1026]{2,1,0:T(1,128)} %get-tuple-element.423), channel_id=1, source_target_pairs={{0,1},{1,2},{2,3},{3,4},{4,5},{5,6},{6,7},{7,8},{8,9},{9,10},{10,1... | collective-permute-start | bytes 295496 | tf_op jit(solution)/shard_map/while/body/eval_jaxpr/ppermute | solution.py:20
  402.1 11.2 %collective-permute-start = (f32[24,8,1]{2,1,0:T(8,128)S(1)}, f32[24,8,1]{2,1,0:T(8,128)S(1)}, u32[]{:S(2)}, u32[]{:S(2)}) collective-permute-start(f32[24,8,1]{2,1,0:T(8,128)S(1)} %get-tuple-element.412), channel_id=1, source_target_pairs={{64,0},{128,64},{192,128},{65,1},{129,65},{193,129},{66,2},{130,66... | collective-permute-start | bytes 2312 | tf_op jit(solution)/shard_map/while/body/eval_jaxpr/ppermute | solution.py:22
  404.0 9.3 %collective-permute-start.1 = (f32[24,8,1]{2,1,0:T(8,128)S(1)}, f32[24,8,1]{2,1,0:T(8,128)S(1)}, u32[]{:S(2)}, u32[]{:S(2)}) collective-permute-start(f32[24,8,1]{2,1,0:T(8,128)S(1)} %get-tuple-element.414), channel_id=1, source_target_pairs={{0,64},{64,128},{128,192},{1,65},{65,129},{129,193},{2,66},{66,130... | collective-permute-start | bytes 2312 | tf_op jit(solution)/shard_map/while/body/eval_jaxpr/ppermute | solution.py:20
  424.4 9.3 %collective-permute-start.4 = (f32[24,8,1]{2,1,0:T(8,128)S(1)}, f32[24,8,1]{2,1,0:T(8,128)}, u32[]{:S(2)}, u32[]{:S(2)}) collective-permute-start(f32[24,8,1]{2,1,0:T(8,128)S(1)} %get-tuple-element.420), channel_id=1, source_target_pairs={{64,0},{128,64},{192,128},{65,1},{129,65},{193,129},{66,2},{130,66... | collective-permute-start | bytes 2312 | tf_op jit(solution)/shard_map/while/body/eval_jaxpr/ppermute | solution.py:22
  438.7 10.3 %collective-permute-start.6 = (f32[24,1,1026]{2,1,0:T(1,128)}, f32[24,1,1026]{2,1,0:T(1,128)}, u32[]{:S(2)}, u32[]{:S(2)}) collective-permute-start(f32[24,1,1026]{2,1,0:T(1,128)} %get-tuple-element.422), channel_id=1, source_target_pairs={{1,0},{2,1},{3,2},{4,3},{5,4},{6,5},{7,6},{8,7},{9,8},{10,9},{11,1... | collective-permute-start | bytes 295496 | tf_op jit(solution)/shard_map/while/body/eval_jaxpr/ppermute | solution.py:22
  440.0 10.8 %collective-permute-start.7 = (f32[24,1,1026]{2,1,0:T(1,128)}, f32[24,1,1026]{2,1,0:T(1,128)}, u32[]{:S(2)}, u32[]{:S(2)}) collective-permute-start(f32[24,1,1026]{2,1,0:T(1,128)} %get-tuple-element.423), channel_id=1, source_target_pairs={{0,1},{1,2},{2,3},{3,4},{4,5},{5,6},{6,7},{7,8},{8,9},{9,10},{10,1... | collective-permute-start | bytes 295496 | tf_op jit(solution)/shard_map/while/body/eval_jaxpr/ppermute | solution.py:20
  458.7 11.2 %collective-permute-start = (f32[24,8,1]{2,1,0:T(8,128)S(1)}, f32[24,8,1]{2,1,0:T(8,128)S(1)}, u32[]{:S(2)}, u32[]{:S(2)}) collective-permute-start(f32[24,8,1]{2,1,0:T(8,128)S(1)} %get-tuple-element.412), channel_id=1, source_target_pairs={{64,0},{128,64},{192,128},{65,1},{129,65},{193,129},{66,2},{130,66... | collective-permute-start | bytes 2312 | tf_op jit(solution)/shard_map/while/body/eval_jaxpr/ppermute | solution.py:22
  460.6 9.3 %collective-permute-start.1 = (f32[24,8,1]{2,1,0:T(8,128)S(1)}, f32[24,8,1]{2,1,0:T(8,128)S(1)}, u32[]{:S(2)}, u32[]{:S(2)}) collective-permute-start(f32[24,8,1]{2,1,0:T(8,128)S(1)} %get-tuple-element.414), channel_id=1, source_target_pairs={{0,64},{64,128},{128,192},{1,65},{65,129},{129,193},{2,66},{66,130... | collective-permute-start | bytes 2312 | tf_op jit(solution)/shard_map/while/body/eval_jaxpr/ppermute | solution.py:20
  481.0 9.3 %collective-permute-start.4 = (f32[24,8,1]{2,1,0:T(8,128)S(1)}, f32[24,8,1]{2,1,0:T(8,128)}, u32[]{:S(2)}, u32[]{:S(2)}) collective-permute-start(f32[24,8,1]{2,1,0:T(8,128)S(1)} %get-tuple-element.420), channel_id=1, source_target_pairs={{64,0},{128,64},{192,128},{65,1},{129,65},{193,129},{66,2},{130,66... | collective-permute-start | bytes 2312 | tf_op jit(solution)/shard_map/while/body/eval_jaxpr/ppermute | solution.py:22
  495.3 11.4 %collective-permute-start.6 = (f32[24,1,1026]{2,1,0:T(1,128)}, f32[24,1,1026]{2,1,0:T(1,128)}, u32[]{:S(2)}, u32[]{:S(2)}) collective-permute-start(f32[24,1,1026]{2,1,0:T(1,128)} %get-tuple-element.422), channel_id=1, source_target_pairs={{1,0},{2,1},{3,2},{4,3},{5,4},{6,5},{7,6},{8,7},{9,8},{10,9},{11,1... | collective-permute-start | bytes 295496 | tf_op jit(solution)/shard_map/while/body/eval_jaxpr/ppermute | solution.py:22
  496.6 10.9 %collective-permute-start.7 = (f32[24,1,1026]{2,1,0:T(1,128)}, f32[24,1,1026]{2,1,0:T(1,128)}, u32[]{:S(2)}, u32[]{:S(2)}) collective-permute-start(f32[24,1,1026]{2,1,0:T(1,128)} %get-tuple-element.423), channel_id=1, source_target_pairs={{0,1},{1,2},{2,3},{3,4},{4,5},{5,6},{6,7},{7,8},{8,9},{9,10},{10,1... | collective-permute-start | bytes 295496 | tf_op jit(solution)/shard_map/while/body/eval_jaxpr/ppermute | solution.py:20
  515.4 12.2 %collective-permute-start = (f32[24,8,1]{2,1,0:T(8,128)S(1)}, f32[24,8,1]{2,1,0:T(8,128)S(1)}, u32[]{:S(2)}, u32[]{:S(2)}) collective-permute-start(f32[24,8,1]{2,1,0:T(8,128)S(1)} %get-tuple-element.412), channel_id=1, source_target_pairs={{64,0},{128,64},{192,128},{65,1},{129,65},{193,129},{66,2},{130,66... | collective-permute-start | bytes 2312 | tf_op jit(solution)/shard_map/while/body/eval_jaxpr/ppermute | solution.py:22
  517.4 10.3 %collective-permute-start.1 = (f32[24,8,1]{2,1,0:T(8,128)S(1)}, f32[24,8,1]{2,1,0:T(8,128)S(1)}, u32[]{:S(2)}, u32[]{:S(2)}) collective-permute-start(f32[24,8,1]{2,1,0:T(8,128)S(1)} %get-tuple-element.414), channel_id=1, source_target_pairs={{0,64},{64,128},{128,192},{1,65},{65,129},{129,193},{2,66},{66,130... | collective-permute-start | bytes 2312 | tf_op jit(solution)/shard_map/while/body/eval_jaxpr/ppermute | solution.py:20
  538.7 10.6 %collective-permute-start.4 = (f32[24,8,1]{2,1,0:T(8,128)S(1)}, f32[24,8,1]{2,1,0:T(8,128)}, u32[]{:S(2)}, u32[]{:S(2)}) collective-permute-start(f32[24,8,1]{2,1,0:T(8,128)S(1)} %get-tuple-element.420), channel_id=1, source_target_pairs={{64,0},{128,64},{192,128},{65,1},{129,65},{193,129},{66,2},{130,66... | collective-permute-start | bytes 2312 | tf_op jit(solution)/shard_map/while/body/eval_jaxpr/ppermute | solution.py:22
  (72 other events, 430.5 us)
where the time goes:
time: 734 us; the launch traced here: 727 us
  starting transfers between devices  313 us (43%)
  other arithmetic  151 us (21%)
  blocking collectives  128 us (17%)
  local copies, waits for them, and re-layouts  92.8 us (13%)
  waiting for transfers between devices  35.7 us (5%)
    ppermute x42, starting transfers between devices, padded_2(): lax.ppermute(tail, axis, [(i, (i + 1) % count) for i in range(ends)])  243 us
    psum x1, blocking collectives, body(): total = lax.psum(local, ('sec', 'dom'))  128 us
    ppermute x42, starting transfers between devices, padded_2(): lax.ppermute(head, axis, [((i + 1) % count, i) for i in range(ends)])  70.7 us
    another operation x20, other arithmetic, pair_step(): jnp.stack([position * cells, velocity * cells], 1).astype(jnp.bfloat16)  56.7 us
    ppermute x42, waiting for transfers between devices, padded_2(): lax.ppermute(tail, axis, [(i, (i + 1) % count) for i in range(ends)])  35 us
    mul x20, other arithmetic, divergence(): total = total + 0.5 * (stiff_centre + stiff_near) * (nearby - centre)  28 us
    concatenate x21, local copies, waits for them, and re-layouts, padded_2(): jnp.concatenate([lax.ppermute(tail, axis, [(i, (i + 1) % count) for i in...  27.5 us
    slice x40, local copies, waits for them, and re-layouts, padded_2(): lax.slice_in_dim(cells, cells.shape[dim] - width, cells.shape[dim], axis=...  26.8 us
  transfers between devices with their start and end apart: 84, of which 32 were waited for; matrix products, arithmetic and copies ran while one was open for 8% of the time, Pallas kernels for 0%

commit v1 on v0

--- a/solution.py
+++ b/solution.py
@@ -85,7 +85,7 @@
         primal, adjoint, (((1,), (1,)), ((), ())), preferred_element_type=jnp.float32
     )
     factor = 1.0 / math.sqrt(rows * cols * lax.axis_size("sec") * lax.axis_size("dom"))
-    total = lax.psum(local, ("sec", "dom"))
+    total = lax.psum(lax.psum(local, "sec"), "dom")
     share = local.shape[0] // lax.axis_size("sec")
     block = lax.dynamic_slice_in_dim(total, lax.axis_index("sec") * share, share, 0)
     return (position, block * factor)

time: 734 us -> 961 us (1.31)
  the two profiles are of different devices: /device:TPU:1 before, /device:TPU:4 now
where the time goes in v1:
time: 961 us; the launch traced here: 954 us
  blocking collectives  354 us (37%)
  starting transfers between devices  258 us (27%)
  other arithmetic  150 us (16%)
  waiting for transfers between devices  92.9 us (10%)
  local copies, waits for them, and re-layouts  92.5 us (10%)
    psum x2, blocking collectives, body(): total = lax.psum(lax.psum(local, 'sec'), 'dom')  354 us
    ppermute x42, starting transfers between devices, padded_2(): lax.ppermute(tail, axis, [(i, (i + 1) % count) for i in range(ends)])  191 us
    ppermute x42, waiting for transfers between devices, padded_2(): lax.ppermute(tail, axis, [(i, (i + 1) % count) for i in range(ends)])  91.3 us
    ppermute x42, starting transfers between devices, padded_2(): lax.ppermute(head, axis, [((i + 1) % count, i) for i in range(ends)])  67.3 us
    another operation x20, other arithmetic, pair_step(): jnp.stack([position * cells, velocity * cells], 1).astype(jnp.bfloat16)  56.3 us
    mul x20, other arithmetic, divergence(): total = total + 0.5 * (stiff_centre + stiff_near) * (nearby - centre)  28.2 us
    concatenate x21, local copies, waits for them, and re-layouts, padded_2(): jnp.concatenate([lax.ppermute(tail, axis, [(i, (i + 1) % count) for i in...  27.5 us
    slice x40, local copies, waits for them, and re-layouts, padded_2(): lax.slice_in_dim(cells, cells.shape[dim] - width, cells.shape[dim], axis=...  27.2 us
  transfers between devices with their start and end apart: 84, of which 43 were waited for; matrix products, arithmetic and copies ran while one was open for 6% of the time, Pallas kernels for 0%

profile of v1, /device:TPU:4, one launch (start us, length us, event | category | flops | bytes accessed | tf_op | source)
XLA Modules:
  0.0 953.9 jit_solution(26046953882501818)
XLA Ops:
  19.3 552.3 %while.20 = (s32[]{:T(128)}, f32[24,8,1024]{2,1,0:T(8,128)}, f32[24,8,1024]{2,1,0:T(8,128)S(1)}, bf16[24,10,2,8,1024]{4,3,0,2,1:T(8,128)(2,1)}, f32[8,1024]{1,0:...) while((s32[]{:T(128)}, f32[24,8,1024]{2,1,0:T(8,128)}, ...), condition=%wide.region_3.4_spmd.clone, body=%wide.region_2.3_spmd.clone.sunk | while | flops 13410315 | bytes 20697064 | solution.py:80
  30.7 5.5 collective-permute-start.3
  57.0 6.0 collective-permute-start.7
  65.5 5.6 fusion.52
  84.6 5.4 collective-permute-start.3
  111.2 6.3 collective-permute-start.7
  119.7 5.6 fusion.52
  138.9 5.8 collective-permute-start.3
  165.4 6.3 collective-permute-start.7
  173.9 5.6 fusion.52
  193.1 6.7 collective-permute-start.3
  220.5 6.0 collective-permute-start.7
  229.0 5.6 fusion.52
  248.2 5.4 collective-permute-start.3
  274.7 6.3 collective-permute-start.7
  283.2 5.6 fusion.52
  302.4 5.4 collective-permute-start.3
  329.5 6.3 collective-permute-start.7
  338.0 5.6 fusion.52
  383.2 9.2 collective-permute-start.7
  394.6 5.6 fusion.52
  439.8 9.2 collective-permute-start.7
  451.2 5.6 fusion.52
  470.4 5.4 collective-permute-start.3
  496.4 10.4 %collective-permute-start.7 = (f32[24,1,1026]{2,1,0:T(1,128)}, f32[24,1,1026]{2,1,0:T(1,128)}, u32[]{:S(2)}, u32[]{:S(2)}) collective-permute-start(f32[24,1,1026]{2,1,0:T(1,128)} %get-tuple-element.423), channel_id=1, source_target_pairs={{0,1},{1,2},{2,3},{3,4},{4,5},{5,6},{6,7},{7,8},{8,9},{9,10},{10,1... | collective-permute-start | bytes 295496 | tf_op jit(solution)/shard_map/while/body/eval_jaxpr/ppermute | solution.py:20
  508.9 5.6 fusion.52
  528.1 5.6 collective-permute-start.3
  555.5 7.4 collective-permute-start.7
  565.0 5.6 fusion.52
  580.2 8.9 slice.229
  598.8 14.0 %psum.14 = f32[160,80]{1,0:T(8,128)S(1)} all-reduce(f32[160,80]{1,0:T(8,128)S(1)} %fusion.39), channel_id=1, replica_groups=mesh['sec'=4,'dom'=64] {'sec'}, use_global_device_ids=true, to_apply=%region_4.5 | all-reduce | flops 12800 | bytes 102400 | tf_op jit(solution)/shard_map/psum | solution.py:88
  612.8 340.5 %psum.15 = f32[160,80]{1,0:T(8,128)S(1)} all-reduce(f32[160,80]{1,0:T(8,128)S(1)} %psum.14), channel_id=1, replica_groups=mesh['sec'=4,'dom'=64] {'dom'}, use_global_device_ids=true, to_apply=%region_5.6 | all-reduce | flops 12800 | bytes 102400 | tf_op jit(solution)/shard_map/psum | solution.py:88
  (357 shorter events, 414.5 us)
Async XLA Ops:
  10.1 8.4 collective-permute-start.11
  30.7 7.9 collective-permute-start.3
  55.7 8.0 collective-permute-start.6
  57.0 8.5 collective-permute-start.7
  84.6 8.2 collective-permute-start.3
  109.9 8.3 collective-permute-start.6
  111.2 8.5 collective-permute-start.7
  137.6 7.9 collective-permute-start.2
  138.9 8.2 collective-permute-start.3
  164.1 8.3 collective-permute-start.6
  165.4 8.5 collective-permute-start.7
  191.8 8.9 collective-permute-start.2
  193.1 9.1 collective-permute-start.3
  219.2 8.0 collective-permute-start.6
  220.5 8.5 collective-permute-start.7
  246.9 8.6 collective-permute-start.2
  248.2 8.2 collective-permute-start.3
  273.4 8.3 collective-permute-start.6
  274.7 8.5 collective-permute-start.7
  302.4 8.8 collective-permute-start.3
  328.2 8.3 collective-permute-start.6
  329.5 8.5 collective-permute-start.7
  357.1 7.7 collective-permute-start.3
  381.9 11.2 %collective-permute-start.6 = (f32[24,1,1026]{2,1,0:T(1,128)}, f32[24,1,1026]{2,1,0:T(1,128)}, u32[]{:S(2)}, u32[]{:S(2)}) collective-permute-start(f32[24,1,1026]{2,1,0:T(1,128)} %get-tuple-element.422), channel_id=1, source_target_pairs={{1,0},{2,1},{3,2},{4,3},{5,4},{6,5},{7,6},{8,7},{9,8},{10,9},{11,1... | collective-permute-start | bytes 295496 | tf_op jit(solution)/shard_map/while/body/eval_jaxpr/ppermute | solution.py:22
  383.2 11.4 %collective-permute-start.7 = (f32[24,1,1026]{2,1,0:T(1,128)}, f32[24,1,1026]{2,1,0:T(1,128)}, u32[]{:S(2)}, u32[]{:S(2)}) collective-permute-start(f32[24,1,1026]{2,1,0:T(1,128)} %get-tuple-element.423), channel_id=1, source_target_pairs={{0,1},{1,2},{2,3},{3,4},{4,5},{5,6},{6,7},{7,8},{8,9},{9,10},{10,1... | collective-permute-start | bytes 295496 | tf_op jit(solution)/shard_map/while/body/eval_jaxpr/ppermute | solution.py:20
  438.5 11.2 %collective-permute-start.6 = (f32[24,1,1026]{2,1,0:T(1,128)}, f32[24,1,1026]{2,1,0:T(1,128)}, u32[]{:S(2)}, u32[]{:S(2)}) collective-permute-start(f32[24,1,1026]{2,1,0:T(1,128)} %get-tuple-element.422), channel_id=1, source_target_pairs={{1,0},{2,1},{3,2},{4,3},{5,4},{6,5},{7,6},{8,7},{9,8},{10,9},{11,1... | collective-permute-start | bytes 295496 | tf_op jit(solution)/shard_map/while/body/eval_jaxpr/ppermute | solution.py:22
  439.8 11.4 %collective-permute-start.7 = (f32[24,1,1026]{2,1,0:T(1,128)}, f32[24,1,1026]{2,1,0:T(1,128)}, u32[]{:S(2)}, u32[]{:S(2)}) collective-permute-start(f32[24,1,1026]{2,1,0:T(1,128)} %get-tuple-element.423), channel_id=1, source_target_pairs={{0,1},{1,2},{2,3},{3,4},{4,5},{5,6},{6,7},{7,8},{8,9},{9,10},{10,1... | collective-permute-start | bytes 295496 | tf_op jit(solution)/shard_map/while/body/eval_jaxpr/ppermute | solution.py:20
  495.1 12.4 %collective-permute-start.6 = (f32[24,1,1026]{2,1,0:T(1,128)}, f32[24,1,1026]{2,1,0:T(1,128)}, u32[]{:S(2)}, u32[]{:S(2)}) collective-permute-start(f32[24,1,1026]{2,1,0:T(1,128)} %get-tuple-element.422), channel_id=1, source_target_pairs={{1,0},{2,1},{3,2},{4,3},{5,4},{6,5},{7,6},{8,7},{9,8},{10,9},{11,1... | collective-permute-start | bytes 295496 | tf_op jit(solution)/shard_map/while/body/eval_jaxpr/ppermute | solution.py:22
  496.4 12.5 %collective-permute-start.7 = (f32[24,1,1026]{2,1,0:T(1,128)}, f32[24,1,1026]{2,1,0:T(1,128)}, u32[]{:S(2)}, u32[]{:S(2)}) collective-permute-start(f32[24,1,1026]{2,1,0:T(1,128)} %get-tuple-element.423), channel_id=1, source_target_pairs={{0,1},{1,2},{2,3},{3,4},{4,5},{5,6},{6,7},{7,8},{8,9},{9,10},{10,1... | collective-permute-start | bytes 295496 | tf_op jit(solution)/shard_map/while/body/eval_jaxpr/ppermute | solution.py:20
  528.1 9.0 collective-permute-start.3
  554.2 9.4 collective-permute-start.6
  555.5 9.5 collective-permute-start.7
  (72 other events, 423.0 us)
